TPU v7x, 128 devices: a whole 4x4x4 slice. The times are simulated.
128 devices in a mesh: row: 16 (over y, x), col: 8 (over z, core).
Axes of the slice: x: 4, y: 4, z: 4, core: 2. Of those that a mesh axis runs over, the one named last changes fastest.
Arguments:
- layer_input: bfloat16 [768, 8192], P('col', 'row'), may hold values from -6 to 6
- out_grad: bfloat16 [768, 8192], P('col', 'row'), may hold values from -6 to 6
- gate_weight: bfloat16 [8192, 28672], P('row', 'col'), may hold values from -0.0625 to 0.0625
- up_weight: bfloat16 [8192, 28672], P('row', 'col'), may hold values from -0.0625 to 0.0625
- down_weight: bfloat16 [28672, 8192], P('col', 'row'), may hold values from -0.03125 to 0.03125
Outputs:
- input_grad: bfloat16 [768, 8192], P('col', 'row')
- gate_grad: bfloat16 [8192, 28672], P('row', 'col')
- up_grad: bfloat16 [8192, 28672], P('row', 'col')
- down_grad: bfloat16 [28672, 8192], P('col', 'row')
All inputs are finite; a program needn't handle non-finite values.
Results may differ from a plain program's by a relative error of at most 0.033.
Values may be sent and summed in bfloat16 or wider, within the bound.
A program may use at most 192 MiB of HBM per device.

v0:
```python
import jax
import jax.numpy as jnp
from jax import lax
from jax.sharding import PartitionSpec as P


def swiglu_back(summed, width):
    gate = summed[:, :width]
    up = summed[:, width : 2 * width]
    hidden_grad = summed[:, 2 * width :]
    sigma = jax.nn.sigmoid(gate)
    swish = gate * sigma
    hidden = (swish * up).astype(jnp.bfloat16)
    up_delta = (hidden_grad * swish).astype(jnp.bfloat16)
    gate_delta = (hidden_grad * up * sigma * (1.0 + gate * (1.0 - sigma))).astype(jnp.bfloat16)
    return (hidden, gate_delta, up_delta)


def local(layer_input, out_grad, gate_weight, up_weight, down_weight):
    input_rows, cot_rows = (
        lax.all_gather(layer_input, "col", axis=0, tiled=True),
        lax.all_gather(out_grad, "col", axis=0, tiled=True),
    )
    tokens = input_rows.shape[0]
    width = gate_weight.shape[1]
    both_weights = jnp.concatenate([gate_weight, up_weight], axis=1)
    contract_last = (((1,), (1,)), ((), ()))
    contract_first = (((0,), (0,)), ((), ()))
    left = input_rows
    right = cot_rows
    gate_up = jnp.dot(left, both_weights, preferred_element_type=jnp.float32)
    hidden_grad = lax.dot_general(
        right, down_weight, contract_last, preferred_element_type=jnp.float32
    )
    summed = lax.psum_scatter(
        jnp.concatenate([gate_up, hidden_grad], axis=1).astype(jnp.bfloat16),
        "row",
        scatter_dimension=0,
        tiled=True,
    ).astype(jnp.float32)
    hidden, gate_delta, up_delta = swiglu_back(summed, width)
    accumulate_hidden = lax.all_gather(hidden, "row", axis=0, tiled=True)
    accumulate_gate_delta = lax.all_gather(gate_delta, "row", axis=0, tiled=True)
    accumulate_up_delta = lax.all_gather(up_delta, "row", axis=0, tiled=True)
    left = input_rows
    right = cot_rows
    down_sum = lax.dot_general(
        accumulate_hidden, right, contract_first, preferred_element_type=jnp.float32
    )
    gate_sum = lax.dot_general(
        left, accumulate_gate_delta, contract_first, preferred_element_type=jnp.float32
    )
    up_sum = lax.dot_general(
        left, accumulate_up_delta, contract_first, preferred_element_type=jnp.float32
    )
    term = lax.dot_general(
        accumulate_gate_delta, gate_weight, contract_last, preferred_element_type=jnp.float32
    )
    term = term + lax.dot_general(
        accumulate_up_delta, up_weight, contract_last, preferred_element_type=jnp.float32
    )
    factor = 1.0 / tokens**0.5
    down_grad = (down_sum * factor).astype(jnp.bfloat16)
    gate_grad = (gate_sum * factor).astype(jnp.bfloat16)
    up_grad = (up_sum * factor).astype(jnp.bfloat16)
    input_grad = lax.psum_scatter(term.astype(jnp.bfloat16), "col", scatter_dimension=0, tiled=True)
    return (input_grad, gate_grad, up_grad, down_grad)


def solution(mesh):
    placed = (P("col", "row"), P("col", "row"), P("row", "col"), P("row", "col"), P("col", "row"))
    return jax.shard_map(
        local,
        mesh=mesh,
        in_specs=placed,
        out_specs=(P("col", "row"), P("row", "col"), P("row", "col"), P("col", "row")),
        check_vma=False,
    )
```

profile of v0, /device:TPU:0, one launch (start us, length us, event | category | flops | bytes accessed | tf_op | source)
XLA Modules:
  0.0 429.2 jit_solution(3540597175312089114)
XLA Ops:
  7.2 0.0 reduce-scatter.7.cloned.1.call-start
  7.2 14.9 %all_gather.15 = bf16[768,512]{1,0:T(8,128)(2,1)S(1)} all-gather(bf16[96,512]{1,0:T(8,128)(2,1)} %param.5), channel_id=1, replica_groups=mesh['row'=16,'col'=8] {'col'}, dimensions={0}, use_global_device_ids=true | all-gather | bytes 884736 | tf_op jit(solution)/shard_map/all_gather | solution.py:21
  22.1 13.6 %all_gather.16 = bf16[768,512]{1,0:T(8,128)(2,1)S(1)} all-gather(bf16[96,512]{1,0:T(8,128)(2,1)} %param.6), channel_id=1, replica_groups=mesh['row'=16,'col'=8] {'col'}, dimensions={0}, use_global_device_ids=true | all-gather | bytes 884736 | tf_op jit(solution)/shard_map/all_gather | solution.py:22
  35.7 7.5 %convolution_convert_fusion.1 = bf16[768,3584]{0,1:T(8,128)(2,1)} fusion(bf16[768,512]{1,0:T(8,128)(2,1)S(1)} %all_gather.16, bf16[3584,512]{1,0:T(8,128)(2,1)} %param.9), kind=kOutput, calls=%fused_computation.9 | convolution fusion | flops 2821324800 | bytes 9961472 | tf_op jit(solution)/shard_map/dot_general | solution.py:32
  43.2 13.8 %fusion = bf16[768,7168]{0,1:T(8,128)(2,1)} fusion(bf16[768,512]{1,0:T(8,128)(2,1)S(1)} %all_gather.15, bf16[512,3584]{1,0:T(8,128)(2,1)} %param.8, bf16[512,3584]{1,0:T(8,128)(2,1)} %param.7), kind=kOutput, calls=%fused_computation.2 | convolution fusion | flops 5657329664 | bytes 19136512 | tf_op jit(solution)/shard_map/dot_general | solution.py:31
  57.0 18.5 %pad_maximum_fusion = bf16[768,10752]{0,1:T(8,128)(2,1)} fusion(bf16[768,3584]{0,1:T(8,128)(2,1)} %convolution_convert_fusion.1, bf16[768,7168]{0,1:T(8,128)(2,1)} %fusion), kind=kLoop, calls=%fused_computation | loop fusion | flops 33030144 | bytes 33030144 | tf_op jit(solution)/shard_map/concatenate | solution.py:36
  75.5 22.3 %copy.23 = bf16[768,10752]{1,0:T(8,128)(2,1)} copy(bf16[768,10752]{0,1:T(8,128)(2,1)} %pad_maximum_fusion) | data formatting | bytes 33030144
  97.8 0.0 reduce-scatter.7.cloned.1.call-update
  97.8 0.0 all-gather.4.cloned.1.call-start
  97.9 110.7 %reduce-scatter.7.cloned.1.call-done = bf16[48,10752]{1,0:T(8,128)(2,1)} async-done(((bf16[768,10752]{1,0:T(8,128)(2,1)}), bf16[48,10752]{1,0:T(8,128)(2,1)}) %reduce-scatter.7.cloned.1.call-update) | async-done | bytes 1032208 | tf_op jit(solution)/shard_map/reduce_scatter | solution.py:35
  208.6 1.4 convert_element_type.31
  210.0 1.3 multiply_convert_fusion.3
  211.3 0.0 all-gather.4.cloned.1.call-update
  211.3 0.0 all-gather.6.cloned.1.call-start
  211.3 0.7 all-gather.6.cloned.1.call-update
  212.0 0.0 all-gather.8.cloned.1.call-start
  212.1 0.5 all-gather.8.cloned.1.call-update
  212.6 0.2 reduce-scatter.5.cloned.1.call-start
  212.8 55.8 %all-gather.4.cloned.1.call-done = bf16[768,3584]{1,0:T(8,128)(2,1)} async-done(((bf16[48,3584]{1,0:T(8,128)(2,1)}), bf16[768,3584]{1,0:T(8,128)(2,1)}) %all-gather.4.cloned.1.call-update) | async-done | bytes 5505040 | tf_op jit(solution)/shard_map/all_gather | solution.py:43
  268.6 6.1 %fusion.8 = f32[768,512]{1,0:T(8,128)S(1)} fusion(bf16[768,3584]{1,0:T(8,128)(2,1)} %all-gather.4.cloned.1.call-done, bf16[512,3584]{1,0:T(8,128)(2,1)} %param.7), kind=kOutput, calls=%fused_computation.19 | convolution fusion | flops 2818572288 | bytes 10747904 | tf_op jit(solution)/shard_map/dot_general | solution.py:56
  274.8 54.1 %all-gather.6.cloned.1.call-done = bf16[768,3584]{1,0:T(8,128)(2,1)} async-done(((bf16[48,3584]{1,0:T(8,128)(2,1)}), bf16[768,3584]{1,0:T(8,128)(2,1)}) %all-gather.6.cloned.1.call-update) | async-done | bytes 5505040 | tf_op jit(solution)/shard_map/all_gather | solution.py:44
  328.8 7.6 %add_convert_fusion = bf16[768,512]{1,0:T(8,128)(2,1)} fusion(f32[768,512]{1,0:T(8,128)S(1)} %fusion.8, bf16[768,3584]{1,0:T(8,128)(2,1)} %all-gather.6.cloned.1.call-done, bf16[512,3584]{1,0:T(8,128)(2,1)} %param.8), kind=kOutput, calls=%fused_computation.12 | convolution fusion | flops 2819358720 | bytes 11534336 | tf_op jit(solution)/shard_map/dot_general | solution.py:59
  336.4 0.0 reduce-scatter.5.cloned.1.call-update
  336.5 7.1 %fusion.5 = bf16[512,3584]{0,1:T(8,128)(2,1)} fusion(bf16[768,3584]{1,0:T(8,128)(2,1)} %all-gather.6.cloned.1.call-done, bf16[768,512]{1,0:T(8,128)(2,1)S(1)} %all_gather.15), kind=kOutput, calls=%fused_computation.11 | convolution fusion | flops 2822242304 | bytes 9961472 | tf_op jit(solution)/shard_map/dot_general | solution.py:53
  343.6 5.9 %copy.21 = bf16[512,3584]{1,0:T(8,128)(2,1)} copy(bf16[512,3584]{0,1:T(8,128)(2,1)} %fusion.5) | data formatting | bytes 7340032
  349.5 7.1 %fusion.4 = bf16[512,3584]{0,1:T(8,128)(2,1)} fusion(bf16[768,3584]{1,0:T(8,128)(2,1)} %all-gather.4.cloned.1.call-done, bf16[768,512]{1,0:T(8,128)(2,1)S(1)} %all_gather.15), kind=kOutput, calls=%fused_computation.10 | convolution fusion | flops 2822242304 | bytes 9961472 | tf_op jit(solution)/shard_map/dot_general | solution.py:50
  356.6 5.9 %copy.20 = bf16[512,3584]{1,0:T(8,128)(2,1)} copy(bf16[512,3584]{0,1:T(8,128)(2,1)} %fusion.4) | data formatting | bytes 7340032
  362.5 25.8 %all-gather.8.cloned.1.call-done = bf16[768,3584]{1,0:T(8,128)(2,1)} async-done(((bf16[48,3584]{1,0:T(8,128)(2,1)}), bf16[768,3584]{1,0:T(8,128)(2,1)}) %all-gather.8.cloned.1.call-update) | async-done | bytes 5505040 | tf_op jit(solution)/shard_map/all_gather | solution.py:42
  388.3 7.1 %multiply_convert_fusion = bf16[3584,512]{1,0:T(8,128)(2,1)} fusion(bf16[768,3584]{1,0:T(8,128)(2,1)} %all-gather.8.cloned.1.call-done, bf16[768,512]{1,0:T(8,128)(2,1)S(1)} %all_gather.16), kind=kOutput, calls=%fused_computation.6 | convolution fusion | flops 2822242304 | bytes 9961472 | tf_op jit(solution)/shard_map/dot_general | solution.py:47
  395.4 27.2 %reduce-scatter.5.cloned.1.call-done = bf16[96,512]{1,0:T(8,128)(2,1)} async-done(((bf16[768,512]{1,0:T(8,128)(2,1)}), bf16[96,512]{1,0:T(8,128)(2,1)}) %reduce-scatter.5.cloned.1.call-update) | async-done | bytes 98320 | tf_op jit(solution)/shard_map/reduce_scatter | solution.py:66
Async XLA Ops:
  7.2 201.5 %reduce-scatter.7.cloned.1.call-start = ((), (), s32[]{:S(2)}) async-start(), calls=%async_computation.6 | async-start | bytes 17547264 | tf_op jit(solution)/shard_map/reduce_scatter | solution.py:35
  97.8 170.8 %all-gather.4.cloned.1.call-start = ((), (), s32[]{:S(2)}) async-start(), calls=%async_computation.2 | async-start | bytes 5849088 | tf_op jit(solution)/shard_map/all_gather | solution.py:43
  211.3 117.5 %all-gather.6.cloned.1.call-start = ((), (), s32[]{:S(2)}) async-start(), calls=%async_computation.3 | async-start | bytes 5849088 | tf_op jit(solution)/shard_map/all_gather | solution.py:44
  212.0 176.3 %all-gather.8.cloned.1.call-start = ((), (), s32[]{:S(2)}) async-start(), calls=%async_computation.5 | async-start | bytes 5849088 | tf_op jit(solution)/shard_map/all_gather | solution.py:42
  212.6 210.0 %reduce-scatter.5.cloned.1.call-start = ((), (), s32[]{:S(2)}) async-start(), calls=%async_computation.4 | async-start | bytes 884736 | tf_op jit(solution)/shard_map/reduce_scatter | solution.py:66
Sparse Core Ops, SparseCore 0:
  98.0 110.6 reduce-scatter.6
  211.6 57.0 all-gather.3
  271.6 57.2 all-gather.5
  331.1 57.2 all-gather.7
  391.3 31.3 reduce-scatter.4
where the time goes:
time: 430 us; the launch traced here: 429 us
  waiting for transfers between devices  275 us (64%)
  matrix products  56.3 us (13%)
  local copies, waits for them, and re-layouts  34.2 us (8%)
  blocking collectives  28.5 us (7%)
  other arithmetic  21.2 us (5%)
  between operations  13.8 us (3%)
    reduce_scatter x1, waiting for transfers between devices, local(): lax.psum_scatter(jnp.concatenate([gate_up, hidden_grad], axis=1).astype(j...  111 us
    all_gather x1, waiting for transfers between devices, local(): lax.all_gather(gate_delta, 'row', axis=0, tiled=True)  55.8 us
    all_gather x1, waiting for transfers between devices, local(): accumulate_up_delta = lax.all_gather(up_delta, 'row', axis=0, tiled=True)  54.1 us
    unnamed x3, local copies, waits for them, and re-layouts  34.2 us
    reduce_scatter x1, waiting for transfers between devices, local(): lax.psum_scatter(term.astype(jnp.bfloat16), 'col', scatter_dimension=0, t...  27.2 us
    all_gather x1, waiting for transfers between devices, local(): accumulate_hidden = lax.all_gather(hidden, 'row', axis=0, tiled=True)  25.8 us
    concatenate x1, other arithmetic, local(): jnp.concatenate([gate_up, hidden_grad], axis=1).astype(jnp.bfloat16)  18.5 us
    all_gather x1, blocking collectives, local(): lax.all_gather(layer_input, 'col', axis=0, tiled=True)  14.9 us
  transfers between devices with their start and end apart: 5, of which 5 were waited for; matrix products, arithmetic and copies ran while one was open for 11% of the time, Pallas kernels for 0%

commit v1 on v0

--- a/solution.py
+++ b/solution.py
@@ -2,6 +2,7 @@
 import jax.numpy as jnp
 from jax import lax
 from jax.sharding import PartitionSpec as P
+from jax.lax import all_gather
 
 
 def swiglu_back(summed, width):
@@ -39,8 +40,12 @@
         tiled=True,
     ).astype(jnp.float32)
     hidden, gate_delta, up_delta = swiglu_back(summed, width)
-    accumulate_hidden = lax.all_gather(hidden, "row", axis=0, tiled=True)
-    accumulate_gate_delta = lax.all_gather(gate_delta, "row", axis=0, tiled=True)
+    _order_lane = lambda chunk, u, axis_tag: jnp.split(
+        all_gather(jnp.concatenate([chunk, u], axis=1), axis_tag, tiled=True, axis=0),
+        [chunk.shape[1]],
+        axis=1,
+    )
+    accumulate_hidden, accumulate_gate_delta = _order_lane(hidden, gate_delta, "row")
     accumulate_up_delta = lax.all_gather(up_delta, "row", axis=0, tiled=True)
     left = input_rows
     right = cot_rows

time: 430 us -> 401 us (0.933)
  waiting for transfers between devices: 275 us -> 243 us
    all_gather x2 -> x1, waiting for transfers between devices: 81.6 us -> 64.2 us  [local(): all_gather(jnp.concatenate([chunk, u], axis=1), axis_tag, tiled=True, axi...]
    reduce_scatter x1, waiting for transfers between devices: 27.2 us -> 11.2 us  [local(): lax.psum_scatter(term.astype(jnp.bfloat16), 'col', scatter_dimension=0, t...]
  transfers between devices with their start and end apart: 5 -> 4, of which waited for: 5 -> 4; matrix products, arithmetic and copies ran while one was open for 11% -> 11% of each run, Pallas kernels for 0% -> 0%
where the time goes in v1:
time: 401 us; the launch traced here: 400 us
  waiting for transfers between devices  243 us (61%)
  matrix products  58.7 us (15%)
  local copies, waits for them, and re-layouts  34.1 us (9%)
  blocking collectives  28.5 us (7%)
  other arithmetic  21.8 us (5%)
  between operations  13.8 us (3%)
    reduce_scatter x1, waiting for transfers between devices, local(): lax.psum_scatter(jnp.concatenate([gate_up, hidden_grad], axis=1).astype(j...  111 us
    all_gather x1, waiting for transfers between devices, local(): all_gather(jnp.concatenate([chunk, u], axis=1), axis_tag, tiled=True, axi...  64.2 us
    all_gather x1, waiting for transfers between devices, local(): accumulate_up_delta = lax.all_gather(up_delta, 'row', axis=0, tiled=True)  56.4 us
    unnamed x3, local copies, waits for them, and re-layouts  34.1 us
    concatenate x1, other arithmetic, local(): jnp.concatenate([gate_up, hidden_grad], axis=1).astype(jnp.bfloat16)  18.5 us
    all_gather x1, blocking collectives, local(): lax.all_gather(layer_input, 'col', axis=0, tiled=True)  14.9 us
    dot_general x1, matrix products, local(): gate_up = jnp.dot(left, both_weights, preferred_element_type=jnp.float32)  13.8 us
    all_gather x1, blocking collectives, local(): lax.all_gather(out_grad, 'col', axis=0, tiled=True)  13.6 us
  transfers between devices with their start and end apart: 4, of which 4 were waited for; matrix products, arithmetic and copies ran while one was open for 11% of the time, Pallas kernels for 0%

profile of v1, /device:TPU:0, one launch (start us, length us, event | category | flops | bytes accessed | tf_op | source)
XLA Modules:
  0.0 399.9 jit_solution(1978704232832963677)
XLA Ops:
  7.2 0.0 reduce-scatter.7.cloned.1.call-start
  7.2 14.9 %all_gather.12 = bf16[768,512]{1,0:T(8,128)(2,1)S(1)} all-gather(bf16[96,512]{1,0:T(8,128)(2,1)} %param.5), channel_id=1, replica_groups=mesh['row'=16,'col'=8] {'col'}, dimensions={0}, use_global_device_ids=true | all-gather | bytes 884736 | tf_op jit(solution)/shard_map/all_gather | solution.py:22
  22.1 13.6 %all_gather.13 = bf16[768,512]{1,0:T(8,128)(2,1)S(1)} all-gather(bf16[96,512]{1,0:T(8,128)(2,1)} %param.6), channel_id=1, replica_groups=mesh['row'=16,'col'=8] {'col'}, dimensions={0}, use_global_device_ids=true | all-gather | bytes 884736 | tf_op jit(solution)/shard_map/all_gather | solution.py:23
  35.7 7.5 %convolution_convert_fusion.1 = bf16[768,3584]{0,1:T(8,128)(2,1)} fusion(bf16[768,512]{1,0:T(8,128)(2,1)S(1)} %all_gather.13, bf16[3584,512]{1,0:T(8,128)(2,1)} %param.9), kind=kOutput, calls=%fused_computation.9 | convolution fusion | flops 2821324800 | bytes 9961472 | tf_op jit(solution)/shard_map/dot_general | solution.py:33
  43.2 13.8 %fusion = bf16[768,7168]{0,1:T(8,128)(2,1)} fusion(bf16[768,512]{1,0:T(8,128)(2,1)S(1)} %all_gather.12, bf16[512,3584]{1,0:T(8,128)(2,1)} %param.8, bf16[512,3584]{1,0:T(8,128)(2,1)} %param.7), kind=kOutput, calls=%fused_computation.2 | convolution fusion | flops 5657329664 | bytes 19136512 | tf_op jit(solution)/shard_map/dot_general | solution.py:32
  57.0 18.5 %pad_maximum_fusion = bf16[768,10752]{0,1:T(8,128)(2,1)} fusion(bf16[768,3584]{0,1:T(8,128)(2,1)} %convolution_convert_fusion.1, bf16[768,7168]{0,1:T(8,128)(2,1)} %fusion), kind=kLoop, calls=%fused_computation | loop fusion | flops 33030144 | bytes 33030144 | tf_op jit(solution)/shard_map/concatenate | solution.py:37
  75.5 22.3 %copy.23 = bf16[768,10752]{1,0:T(8,128)(2,1)} copy(bf16[768,10752]{0,1:T(8,128)(2,1)} %pad_maximum_fusion) | data formatting | bytes 33030144
  97.8 0.0 reduce-scatter.7.cloned.1.call-update
  97.8 0.0 all-gather.5.cloned.1.call-start
  97.8 110.7 %reduce-scatter.7.cloned.1.call-done = bf16[48,10752]{1,0:T(8,128)(2,1)} async-done(((bf16[768,10752]{1,0:T(8,128)(2,1)}), bf16[48,10752]{1,0:T(8,128)(2,1)}) %reduce-scatter.7.cloned.1.call-update) | async-done | bytes 1032208 | tf_op jit(solution)/shard_map/reduce_scatter | solution.py:36
  208.5 1.4 convert_element_type.31
  209.9 1.1 multiply_convert_fusion.5
  211.0 0.0 all-gather.5.cloned.1.call-update
  211.0 0.0 all-gather.3.cloned.1.call-start
  211.0 0.9 pad_maximum_fusion.1
  211.9 0.0 all-gather.3.cloned.1.call-update
  212.0 0.2 reduce-scatter.5.cloned.1.call-start
  212.2 56.4 %all-gather.5.cloned.1.call-done = bf16[768,3584]{1,0:T(8,128)(2,1)} async-done(((bf16[48,3584]{1,0:T(8,128)(2,1)}), bf16[768,3584]{1,0:T(8,128)(2,1)}) %all-gather.5.cloned.1.call-update) | async-done | bytes 5505040 | tf_op jit(solution)/shard_map/all_gather | solution.py:49
  268.6 7.1 %fusion.6 = bf16[512,3584]{0,1:T(8,128)(2,1)} fusion(bf16[768,3584]{1,0:T(8,128)(2,1)} %all-gather.5.cloned.1.call-done, bf16[768,512]{1,0:T(8,128)(2,1)S(1)} %all_gather.12), kind=kOutput, calls=%fused_computation.12 | convolution fusion | flops 2822242304 | bytes 9961472 | tf_op jit(solution)/shard_map/dot_general | solution.py:58
  275.7 5.9 %copy.21 = bf16[512,3584]{1,0:T(8,128)(2,1)} copy(bf16[512,3584]{0,1:T(8,128)(2,1)} %fusion.6) | data formatting | bytes 7340032
  281.6 8.1 %fusion.14 = f32[768,512]{1,0:T(8,128)} fusion(bf16[768,3584]{1,0:T(8,128)(2,1)} %all-gather.5.cloned.1.call-done, bf16[512,3584]{1,0:T(8,128)(2,1)} %param.8), kind=kOutput, calls=%fused_computation.24 | convolution fusion | flops 2818572288 | bytes 10747904 | tf_op jit(solution)/shard_map/dot_general | solution.py:64
  289.6 64.2 %all-gather.3.cloned.1.call-done = bf16[768,7168]{1,0:T(8,128)(2,1)} async-done(((bf16[48,7168]{1,0:T(8,128)(2,1)}), bf16[768,7168]{1,0:T(8,128)(2,1)}) %all-gather.3.cloned.1.call-update) | async-done | bytes 11010064 | tf_op jit(solution)/shard_map/all_gather | solution.py:44
  353.9 8.0 %add_convert_fusion = bf16[768,512]{1,0:T(8,128)(2,1)} fusion(f32[768,512]{1,0:T(8,128)} %fusion.14, bf16[512,3584]{1,0:T(8,128)(2,1)} %param.7, bf16[768,7168]{1,0:T(8,128)(2,1)} %all-gather.3.cloned.1.call-done), kind=kOutput, calls=%fused_computation.16 | convolution fusion | flops 2819358720 | bytes 11534336 | tf_op jit(solution)/shard_map/dot_general | solution.py:61
  361.9 0.0 reduce-scatter.5.cloned.1.call-update
  361.9 7.1 %fusion.5 = bf16[512,3584]{0,1:T(8,128)(2,1)} fusion(bf16[768,512]{1,0:T(8,128)(2,1)S(1)} %all_gather.12, bf16[768,7168]{1,0:T(8,128)(2,1)} %all-gather.3.cloned.1.call-done), kind=kOutput, calls=%fused_computation.11 | convolution fusion | flops 2822242304 | bytes 9961472 | tf_op jit(solution)/shard_map/dot_general | solution.py:55
  369.0 5.9 %copy.20 = bf16[512,3584]{1,0:T(8,128)(2,1)} copy(bf16[512,3584]{0,1:T(8,128)(2,1)} %fusion.5) | data formatting | bytes 7340032
  375.0 7.1 %multiply_convert_fusion = bf16[3584,512]{1,0:T(8,128)(2,1)} fusion(bf16[768,512]{1,0:T(8,128)(2,1)S(1)} %all_gather.13, bf16[768,7168]{1,0:T(8,128)(2,1)} %all-gather.3.cloned.1.call-done), kind=kOutput, calls=%fused_computation.6 | convolution fusion | flops 2822242304 | bytes 9961472 | tf_op jit(solution)/shard_map/dot_general | solution.py:52
  382.1 11.2 %reduce-scatter.5.cloned.1.call-done = bf16[96,512]{1,0:T(8,128)(2,1)} async-done(((bf16[768,512]{1,0:T(8,128)(2,1)}), bf16[96,512]{1,0:T(8,128)(2,1)}) %reduce-scatter.5.cloned.1.call-update) | async-done | bytes 98320 | tf_op jit(solution)/shard_map/reduce_scatter | solution.py:71
Async XLA Ops:
  7.2 201.4 %reduce-scatter.7.cloned.1.call-start = ((), (), s32[]{:S(2)}) async-start(), calls=%async_computation.5 | async-start | bytes 17547264 | tf_op jit(solution)/shard_map/reduce_scatter | solution.py:36
  97.8 170.8 %all-gather.5.cloned.1.call-start = ((), (), s32[]{:S(2)}) async-start(), calls=%async_computation.3 | async-start | bytes 5849088 | tf_op jit(solution)/shard_map/all_gather | solution.py:49
  211.0 142.9 %all-gather.3.cloned.1.call-start = ((), (), s32[]{:S(2)}) async-start(), calls=%async_computation.2 | async-start | bytes 11698176 | tf_op jit(solution)/shard_map/all_gather | solution.py:44
  212.0 181.4 %reduce-scatter.5.cloned.1.call-start = ((), (), s32[]{:S(2)}) async-start(), calls=%async_computation.4 | async-start | bytes 884736 | tf_op jit(solution)/shard_map/reduce_scatter | solution.py:71
Sparse Core Ops, SparseCore 0:
  97.9 110.5 reduce-scatter.6
  211.5 57.0 all-gather.4
  271.5 82.3 all-gather.2
  362.0 31.2 reduce-scatter.4
